TPU v7x, 1024 devices: a whole 8x8x8 slice. The times are simulated.
1024 devices in a mesh: dp: 8 (over x), wide: 16 (over y, core), narrow: 8 (over z).
Axes of the slice: x: 8, y: 8, z: 8, core: 2. Of those that a mesh axis runs over, the one named last changes fastest.
Arguments:
- out_grad: bfloat16 [16384, 2048], P(('dp', 'wide', 'narrow')), may hold values from -6 to 6
- routes: int32 [16384, 8], P(('dp', 'wide', 'narrow')), may hold values from 0 to 127, as said below
- gates: bfloat16 [16384, 8], P(('dp', 'wide', 'narrow')), may hold values from 0.029907227 to 0.59765625
- pre_gate: bfloat16 [8, 128, 256, 768], P('dp', ('wide', 'narrow')), may hold values from -5 to 5
- pre_up: bfloat16 [8, 128, 256, 768], P('dp', ('wide', 'narrow')), may hold values from -5 to 5
- down_weight: bfloat16 [128, 768, 2048], P(('wide', 'narrow')), may hold values from -0.125 to 0.125
Outputs:
- grad_down: bfloat16 [128, 768, 2048], P(('wide', 'narrow'), None, 'dp')
- grad_pre_gate: bfloat16 [8, 128, 256, 768], P('dp', ('wide', 'narrow'))
- grad_pre_up: bfloat16 [8, 128, 256, 768], P('dp', ('wide', 'narrow'))
- grad_gates: float32 [16384, 8], P(('dp', 'wide', 'narrow'))
Inputs may be any that keep to these rules, and one draw needn't show every extreme that they name: `routes`: each token names 8 different experts. The tokens of one device name each expert either 0 or 2 times. In every group some expert is named 2 times by every device of the group.
All inputs are finite; a program needn't handle non-finite values.
Results may differ from a plain program's by a relative error of at most 0.012.
Values may be sent and summed in bfloat16 or wider, within the bound.
A program may use at most 32 MiB of HBM per device.

v0:
```python
import jax
import jax.numpy as jnp
from jax import lax
from jax.sharding import PartitionSpec as P


def shards(out_grad, routes, gates, pre_gate, pre_up, down_weight):
    wide_count = lax.axis_size("wide")
    narrow_count = lax.axis_size("narrow")
    experts = wide_count * narrow_count
    token_count, top_count = routes.shape
    slot_count = pre_gate.shape[2]
    capacity = slot_count // experts
    expert_ids = jnp.arange(experts, dtype=jnp.int32)
    named_hits = (routes[:, :, None] == expert_ids[None, None, :]).astype(jnp.int32)
    hit_counts = jnp.sum(named_hits, axis=1)
    before = jnp.cumsum(hit_counts, axis=0) - hit_counts
    position = jnp.sum(named_hits * before[:, None, :], axis=2)
    target = routes * capacity + position
    slot_ids = jnp.arange(slot_count, dtype=jnp.int32)
    placed = target[:, :, None] == slot_ids[None, None, :]
    choose = jnp.sum(placed.astype(jnp.bfloat16), axis=1)
    outgoing = lax.dot_general(
        choose, out_grad, (((0,), (0,)), ((), ())), preferred_element_type=jnp.float32
    ).astype(jnp.bfloat16)
    gate_out = jnp.sum(
        jnp.where(placed, gates[:, :, None].astype(jnp.float32), 0.0), axis=(0, 1)
    ).astype(jnp.bfloat16)
    outgoing = outgoing.reshape(wide_count, narrow_count, capacity, outgoing.shape[1])
    gate_out = gate_out.reshape(wide_count, narrow_count, capacity)
    incoming, gate_in = (
        lax.all_to_all(
            lax.all_to_all(outgoing, "wide", split_axis=0, concat_axis=0, tiled=True),
            "narrow",
            split_axis=1,
            concat_axis=1,
            tiled=True,
        ),
        lax.all_to_all(
            lax.all_to_all(gate_out, "wide", split_axis=0, concat_axis=0, tiled=True),
            "narrow",
            split_axis=1,
            concat_axis=1,
            tiled=True,
        ),
    )
    routed_rows = incoming.reshape(slot_count, incoming.shape[3])
    gate_col = gate_in.reshape(slot_count).astype(jnp.float32)
    gate_pre = pre_gate[0, 0].astype(jnp.float32)
    up_pre = pre_up[0, 0].astype(jnp.float32)
    weight = down_weight[0]
    sigmoid_a = jax.nn.sigmoid(gate_pre)
    hidden = (gate_pre * sigmoid_a * up_pre).astype(jnp.bfloat16)
    back_prop = lax.dot_general(
        routed_rows, weight, (((1,), (1,)), ((), ())), preferred_element_type=jnp.float32
    )
    slot_grad = jnp.sum(hidden.astype(jnp.float32) * back_prop, axis=1)
    carried = gate_col[:, None] * back_prop
    grad_a = (carried * up_pre * sigmoid_a * (1.0 + gate_pre * (1.0 - sigmoid_a))).astype(
        jnp.bfloat16
    )
    grad_b = (carried * gate_pre * sigmoid_a).astype(jnp.bfloat16)
    scaled = (gate_col[:, None] * hidden.astype(jnp.float32)).astype(jnp.bfloat16)
    partial_value = lax.dot_general(
        scaled, routed_rows, (((0,), (0,)), ((), ())), preferred_element_type=jnp.float32
    )
    grad_down = lax.psum_scatter(partial_value, "dp", scatter_dimension=1, tiled=True).astype(
        jnp.bfloat16
    )
    slot_back = slot_grad.reshape(wide_count, narrow_count, capacity)
    returned = lax.all_to_all(
        lax.all_to_all(slot_back, "wide", split_axis=0, concat_axis=0, tiled=True),
        "narrow",
        split_axis=1,
        concat_axis=1,
        tiled=True,
    )
    grad_gates = jnp.take(returned.reshape(slot_count), target.reshape(-1)).reshape(
        token_count, top_count
    )
    return (grad_down[None], grad_a[None, None], grad_b[None, None], grad_gates)


def solution(mesh):
    placed = (
        P(("dp", "wide", "narrow"), None),
        P(("dp", "wide", "narrow"), None),
        P(("dp", "wide", "narrow"), None),
        P("dp", ("wide", "narrow"), None, None),
        P("dp", ("wide", "narrow"), None, None),
        P(("wide", "narrow"), None, None),
    )
    return jax.shard_map(
        shards,
        mesh=mesh,
        in_specs=placed,
        out_specs=(
            P(("wide", "narrow"), None, "dp"),
            P("dp", ("wide", "narrow"), None, None),
            P("dp", ("wide", "narrow"), None, None),
            P(("dp", "wide", "narrow"), None),
        ),
        check_vma=False,
    )
```

profile of v0, /device:TPU:1, one launch (start us, length us, event | category | flops | bytes accessed | tf_op | source)
XLA Modules:
  0.0 207.4 jit_solution(13804127308005530351)
XLA Ops:
  7.2 0.0 copy-start
  7.2 0.9 copy.65
  8.1 0.1 convert_reduce_fusion
  8.2 0.4 select_reduce_fusion.1
  8.7 0.8 copy.67
  9.4 0.1 select_reduce_fusion
  9.5 0.2 convert_element_type.81
  9.7 0.8 copy.68
  10.5 17.4 %all-to-all-start = ((bf16[16,8,2]{1,2,0:T(2,128)(2,1)}), bf16[16,8,2]{1,2,0:T(2,128)(2,1)S(1)}, u32[]{:S(2)}, u32[]{:S(2)}) async-start(bf16[16,8,2]{1,2,0:T(2,128)(2,1)} %copy.68), calls=%async_computation | async-start | bytes 16384 | tf_op jit(solution)/shard_map/all_to_all | solution.py:40
  27.8 0.1 fusion.31
  28.0 2.3 %convolution_convert_fusion = bf16[256,2048]{1,0:T(8,128)(2,1)} fusion(bf16[16,256]{1,0:T(8,128)(2,1)S(1)} %fusion.31, bf16[16,2048]{1,0:T(8,128)(2,1)} %param.6), kind=kOutput, calls=%fused_computation.3 | convolution fusion | flops 17301504 | bytes 1122304 | tf_op jit(solution)/shard_map/dot_general | solution.py:23
  30.2 2.5 %reshape.95 = bf16[16,8,2,2048]{3,2,1,0:T(2,128)(2,1)} reshape(bf16[256,2048]{1,0:T(8,128)(2,1)} %convolution_convert_fusion) | data formatting | bytes 2097152 | tf_op jit(solution)/shard_map/reshape | solution.py:29
  32.8 2.1 all-to-all-done
  34.9 5.2 %all-to-all-start.2 = ((bf16[16,8,2,2048]{3,2,1,0:T(2,128)(2,1)}), bf16[16,8,2,2048]{3,2,1,0:T(2,128)(2,1)}, u32[]{:S(2)}, u32[]{:S(2)}) async-start(bf16[16,8,2,2048]{3,2,1,0:T(2,128)(2,1)} %reshape.95), calls=%async_computation.2 | async-start | bytes 2097152 | tf_op jit(solution)/shard_map/all_to_all | solution.py:33
  40.1 0.7 copy.69
  40.7 27.4 %all-to-all-done.2 = bf16[16,8,2,2048]{3,2,1,0:T(2,128)(2,1)} async-done(((bf16[16,8,2,2048]{3,2,1,0:T(2,128)(2,1)}), bf16[16,8,2,2048]{3,2,1,0:T(2,128)(2,1)}, u32[]{:S(2)}, u32[]{:S(2)}) %all-to-all-start.2) | async-done | bytes 1048608 | tf_op jit(solution)/shard_map/all_to_all | solution.py:33
  68.2 8.0 %all-to-all-start.1 = ((bf16[16,8,2]{0,2,1:T(2,128)(2,1)}), bf16[16,8,2]{0,2,1:T(2,128)(2,1)S(1)}, u32[]{:S(2)}, u32[]{:S(2)}) async-start(bf16[16,8,2]{0,2,1:T(2,128)(2,1)} %copy.69), calls=%async_computation.1 | async-start | bytes 8192 | tf_op jit(solution)/shard_map/all_to_all | solution.py:39
  76.2 3.1 %copy.72 = bf16[16,8,2,2048]{3,2,0,1:T(2,128)(2,1)} copy(bf16[16,8,2,2048]{3,2,1,0:T(2,128)(2,1)} %all-to-all-done.2) | data formatting | bytes 2097152 | tf_op jit(solution)/shard_map/all_to_all | solution.py:33
  79.3 0.0 copy-start.1
  79.3 3.4 %all-to-all-done.1 = bf16[16,8,2]{0,2,1:T(2,128)(2,1)S(1)} async-done(((bf16[16,8,2]{0,2,1:T(2,128)(2,1)}), bf16[16,8,2]{0,2,1:T(2,128)(2,1)S(1)}, u32[]{:S(2)}, u32[]{:S(2)}) %all-to-all-start.1) | async-done | bytes 544 | tf_op jit(solution)/shard_map/all_to_all | solution.py:39
  82.7 0.0 copy-start.2
  82.7 4.2 %all-to-all-start.3 = ((bf16[16,8,2,2048]{3,2,0,1:T(2,128)(2,1)}), bf16[16,8,2,2048]{3,2,0,1:T(2,128)(2,1)}, u32[]{:S(2)}, u32[]{:S(2)}) async-start(bf16[16,8,2,2048]{3,2,0,1:T(2,128)(2,1)} %copy.72), calls=%async_computation.3 | async-start | bytes 2097152 | tf_op jit(solution)/shard_map/all_to_all | solution.py:32
  86.9 0.0 copy-done.2
  86.9 0.0 reduce-scatter.2.cloned.1.call-start
  87.0 0.7 copy_convert_fusion
  87.7 0.8 copy.71
  88.4 1.0 reshape.100
  89.4 26.8 %all-to-all-done.3 = bf16[16,8,2,2048]{3,2,0,1:T(2,128)(2,1)} async-done(((bf16[16,8,2,2048]{3,2,0,1:T(2,128)(2,1)}), bf16[16,8,2,2048]{3,2,0,1:T(2,128)(2,1)}, u32[]{:S(2)}, u32[]{:S(2)}) %all-to-all-start.3) | async-done | bytes 1048608 | tf_op jit(solution)/shard_map/all_to_all | solution.py:32
  116.2 3.2 %copy.73 = bf16[16,8,2,2048]{3,2,1,0:T(2,128)(2,1)} copy(bf16[16,8,2,2048]{3,2,0,1:T(2,128)(2,1)} %all-to-all-done.3) | data formatting | bytes 2097152 | tf_op jit(solution)/shard_map/all_to_all | solution.py:32
  119.4 2.3 %reshape.96 = bf16[256,2048]{1,0:T(8,128)(2,1)} reshape(bf16[16,8,2,2048]{3,2,1,0:T(2,128)(2,1)} %copy.73) | data formatting | bytes 2097152 | tf_op jit(solution)/shard_map/reshape | solution.py:47
  121.7 0.0 copy-done.1
  121.7 5.1 %fusion.23 = f32[768,2048]{1,0:T(8,128)} fusion(bf16[256,2048]{1,0:T(8,128)(2,1)} %reshape.96, bf16[1,1,256,768]{3,2,1,0:T(8,128)(2,1)S(1)} %copy-done.1, bf16[1,1,256,768]{3,2,1,0:T(8,128)(2,1)} %param.9, f32[256]{0:T(256)S(1)} %reshape.100), kind=kOutput, calls=%fused_computation.32 | convolution fusion | flops 807469056 | bytes 8127488 | tf_op jit(solution)/shard_map/dot_general | solution.py:64
  126.8 0.0 reduce-scatter.2.cloned.1.call-update
  126.9 0.6 reshape.99
  127.5 0.0 copy-done
  127.5 3.7 %multiply_reduce_fusion = (f32[256]{0:T(256)S(1)}, bf16[1,1,256,768]{3,2,1,0:T(8,128)(2,1)}, bf16[1,1,256,768]{3,2,1,0:T(8,128)(2,1)}) fusion(bf16[1,1,256,768]{3,2,1,0:T(8,128)(2,1)S(1)} %copy-done.1, bf16[1,1,256,768]{3,2,1,0:T(8,128)(2,1)} %param.9, f32[256]{0:T(256)S(1)} %reshape.100, bf16[256,2048]{1,0:T(8,128)(2,1)} %reshape.96, ...), kind=kOutput, calls=%fused_computation.29 | convolution fusion | flops 809631488 | bytes 5769216 | tf_op jit(solution)/shard_map/dot_general | solution.py:54
  131.2 0.1 reshape.97
  131.3 0.8 copy.74
  132.1 3.7 %all-to-all-start.4 = ((f32[16,8,2]{1,2,0:T(2,128)}), f32[16,8,2]{1,2,0:T(2,128)S(1)}, u32[]{:S(2)}, u32[]{:S(2)}) async-start(f32[16,8,2]{1,2,0:T(2,128)} %copy.74), calls=%async_computation.5 | async-start | bytes 32768 | tf_op jit(solution)/shard_map/all_to_all | solution.py:72
  135.8 0.7 fusion.32
  136.4 6.7 %all-to-all-done.4 = f32[16,8,2]{1,2,0:T(2,128)S(1)} async-done(((f32[16,8,2]{1,2,0:T(2,128)}), f32[16,8,2]{1,2,0:T(2,128)S(1)}, u32[]{:S(2)}, u32[]{:S(2)}) %all-to-all-start.4) | async-done | bytes 1056 | tf_op jit(solution)/shard_map/all_to_all | solution.py:72
  143.2 0.7 copy.75
  143.8 3.3 %all-to-all-start.5 = ((f32[16,8,2]{0,2,1:T(2,128)}), f32[16,8,2]{0,2,1:T(2,128)S(1)}, u32[]{:S(2)}, u32[]{:S(2)}) async-start(f32[16,8,2]{0,2,1:T(2,128)} %copy.75), calls=%async_computation.6 | async-start | bytes 16384 | tf_op jit(solution)/shard_map/all_to_all | solution.py:71
  147.2 6.5 %all-to-all-done.5 = f32[16,8,2]{0,2,1:T(2,128)S(1)} async-done(((f32[16,8,2]{0,2,1:T(2,128)}), f32[16,8,2]{0,2,1:T(2,128)S(1)}, u32[]{:S(2)}, u32[]{:S(2)}) %all-to-all-start.5) | async-done | bytes 1056 | tf_op jit(solution)/shard_map/all_to_all | solution.py:71
  153.7 0.1 copy.76
  153.8 0.1 reshape.98
  154.0 1.3 gather_fusion
  155.2 0.1 gather.7
  155.3 0.7 copy.77
  156.0 42.6 %reduce-scatter.2.cloned.1.call-done = f32[768,256]{1,0:T(8,128)} async-done(((f32[768,2048]{1,0:T(8,128)}), f32[768,256]{1,0:T(8,128)}) %reduce-scatter.2.cloned.1.call-update) | async-done | bytes 786448 | tf_op jit(solution)/shard_map/reduce_scatter | solution.py:67
  198.6 1.9 convert_bitcast_fusion.2
  (5 shorter events, 0.1 us)
Async XLA Ops:
  7.2 120.3 %copy-start = (bf16[1,768,2048]{2,1,0:T(8,128)(2,1)S(1)}, bf16[1,768,2048]{2,1,0:T(8,128)(2,1)}, u32[]{:S(2)}) copy-start(bf16[1,768,2048]{2,1,0:T(8,128)(2,1)} %param.11) | copy-start | bytes 9437188
  10.5 24.4 %all-to-all-start = ((bf16[16,8,2]{1,2,0:T(2,128)(2,1)}), bf16[16,8,2]{1,2,0:T(2,128)(2,1)S(1)}, u32[]{:S(2)}, u32[]{:S(2)}) async-start(bf16[16,8,2]{1,2,0:T(2,128)(2,1)} %copy.68), calls=%async_computation | async-start | bytes 16384 | tf_op jit(solution)/shard_map/all_to_all | solution.py:40
  34.9 33.3 %all-to-all-start.2 = ((bf16[16,8,2,2048]{3,2,1,0:T(2,128)(2,1)}), bf16[16,8,2,2048]{3,2,1,0:T(2,128)(2,1)}, u32[]{:S(2)}, u32[]{:S(2)}) async-start(bf16[16,8,2,2048]{3,2,1,0:T(2,128)(2,1)} %reshape.95), calls=%async_computation.2 | async-start | bytes 2097152 | tf_op jit(solution)/shard_map/all_to_all | solution.py:33
  68.2 14.5 %all-to-all-start.1 = ((bf16[16,8,2]{0,2,1:T(2,128)(2,1)}), bf16[16,8,2]{0,2,1:T(2,128)(2,1)S(1)}, u32[]{:S(2)}, u32[]{:S(2)}) async-start(bf16[16,8,2]{0,2,1:T(2,128)(2,1)} %copy.69), calls=%async_computation.1 | async-start | bytes 8192 | tf_op jit(solution)/shard_map/all_to_all | solution.py:39
  79.3 42.4 %copy-start.1 = (bf16[1,1,256,768]{3,2,1,0:T(8,128)(2,1)S(1)}, bf16[1,1,256,768]{3,2,1,0:T(8,128)(2,1)}, u32[]{:S(2)}) copy-start(bf16[1,1,256,768]{3,2,1,0:T(8,128)(2,1)} %param.10) | copy-start | bytes 1179652
  82.7 4.2 %copy-start.2 = (bf16[16,8,2]{0,2,1:T(2,128)(2,1)}, bf16[16,8,2]{0,2,1:T(2,128)(2,1)S(1)}, u32[]{:S(2)}) copy-start(bf16[16,8,2]{0,2,1:T(2,128)(2,1)S(1)} %all-to-all-done.1) | copy-start | bytes 1540
  82.7 33.5 %all-to-all-start.3 = ((bf16[16,8,2,2048]{3,2,0,1:T(2,128)(2,1)}), bf16[16,8,2,2048]{3,2,0,1:T(2,128)(2,1)}, u32[]{:S(2)}, u32[]{:S(2)}) async-start(bf16[16,8,2,2048]{3,2,0,1:T(2,128)(2,1)} %copy.72), calls=%async_computation.3 | async-start | bytes 2097152 | tf_op jit(solution)/shard_map/all_to_all | solution.py:32
  86.9 111.7 %reduce-scatter.2.cloned.1.call-start = ((), (), s32[]{:S(2)}) async-start(), calls=%async_computation.7 | async-start | bytes 7077888 | tf_op jit(solution)/shard_map/reduce_scatter | solution.py:67
  132.1 11.1 %all-to-all-start.4 = ((f32[16,8,2]{1,2,0:T(2,128)}), f32[16,8,2]{1,2,0:T(2,128)S(1)}, u32[]{:S(2)}, u32[]{:S(2)}) async-start(f32[16,8,2]{1,2,0:T(2,128)} %copy.74), calls=%async_computation.5 | async-start | bytes 32768 | tf_op jit(solution)/shard_map/all_to_all | solution.py:72
  143.8 9.9 %all-to-all-start.5 = ((f32[16,8,2]{0,2,1:T(2,128)}), f32[16,8,2]{0,2,1:T(2,128)S(1)}, u32[]{:S(2)}, u32[]{:S(2)}) async-start(f32[16,8,2]{0,2,1:T(2,128)} %copy.75), calls=%async_computation.6 | async-start | bytes 16384 | tf_op jit(solution)/shard_map/all_to_all | solution.py:71
Sparse Core Ops, SparseCore 0:
  127.0 71.5 reduce-scatter.1
where the time goes:
time: 208 us; the launch traced here: 207 us
  waiting for transfers between devices  115 us (55%)
  starting transfers between devices  42 us (20%)
  local copies, waits for them, and re-layouts  20.6 us (10%)
  between operations  14.1 us (7%)
  matrix products  11.1 us (5%)
  other arithmetic  4.07 us (2%)
    reduce_scatter x1, waiting for transfers between devices, shards(): lax.psum_scatter(partial_value, 'dp', scatter_dimension=1, tiled=True)  42.6 us
    all_to_all x1, waiting for transfers between devices, shards(): lax.all_to_all(outgoing, 'wide', split_axis=0, concat_axis=0, tiled=True)  27.4 us
    all_to_all x1, waiting for transfers between devices, shards(): lax.all_to_all(lax.all_to_all(outgoing, 'wide', split_axis=0, concat_axis...  26.8 us
    all_to_all x1, starting transfers between devices, shards(): lax.all_to_all(gate_out, 'wide', split_axis=0, concat_axis=0, tiled=True)  17.4 us
    all_to_all x1, starting transfers between devices, shards(): lax.all_to_all(lax.all_to_all(gate_out, 'wide', split_axis=0, concat_axis...  8.05 us
    all_to_all x1, waiting for transfers between devices, shards(): lax.all_to_all(slot_back, 'wide', split_axis=0, concat_axis=0, tiled=True)  6.71 us
    all_to_all x1, waiting for transfers between devices, shards(): lax.all_to_all(lax.all_to_all(slot_back, 'wide', split_axis=0, concat_axi...  6.51 us
    all_to_all x1, starting transfers between devices, shards(): lax.all_to_all(outgoing, 'wide', split_axis=0, concat_axis=0, tiled=True)  5.21 us
  transfers between devices with their start and end apart: 7, of which 7 were waited for; matrix products, arithmetic and copies ran while one was open for 10% of the time, Pallas kernels for 0%

commit v1 on v0

v1 whole, which is shorter than its diff:
```python
import functools

import jax
import jax.numpy as jnp
from jax import lax
from jax.experimental import pallas as pl
from jax.experimental.pallas import tpu as pltpu
from jax.sharding import PartitionSpec as P

MESH = pl.DeviceIdType.MESH
F32 = jnp.float32
BF16 = jnp.bfloat16
LANES = 128
SUBS = 4
AHEAD = 3
NT = (((1,), (1,)), ((), ()))


def iota(shape, dim):
    return lax.broadcasted_iota(jnp.int32, shape, dim)


def kernel(
    dims,
    grads_hbm, routes_ref, gates_ref, gate_hbm, up_hbm, weight_hbm,
    down_out, dgate_out, dup_out, droute_ref,
    gate_v, up_v, weight_v, tokens, table, routes_pad, gates_pad, place,
    hidden, factor_a, factor_b, gathered, tables, choose,
    rows_out, rows_in, gate_send, gate_rows, scaled_t, back_prop,
    part_out, part_in, part_sum, down_v, slot_out, slot_in, pack_out, pack_in,
    load_sem, token_sem, token_send, token_recv, table_send, table_recv,
    rows_send, rows_recv, gates_send, gates_recv, part_send, part_recv,
    slot_send, slot_recv, pack_send, pack_recv, store_sem,
):
    dp, wide, narrow, tok, top, feat, hid, slots = dims
    me_x, me_w, me_n = (lax.axis_index(a) for a in ("dp", "wide", "narrow"))
    right, left = lax.rem(me_x + 1, dp), lax.rem(me_x + dp - 1, dp)
    sub_rows = hid // SUBS
    blocks = hid // LANES

    def columns(step):
        first = lax.rem(me_x + (2 * dp - 1) - step, dp) * (2 * LANES)
        second = lax.rem(me_x + 1 + step, dp) * (2 * LANES) + LANES
        return pl.multiple_of(first, LANES), pl.multiple_of(second, LANES)

    def whole(ref, sem):
        pltpu.make_async_copy(ref, ref, sem).wait()

    for step in range(dp):
        for half, col in enumerate(columns(step)):
            pltpu.make_async_copy(
                grads_hbm.at[:, pl.ds(col, LANES)],
                tokens.at[step, pl.ds(half * tok, tok)],
                token_sem,
            ).start()
    loads = [
        pltpu.make_async_copy(src, dst, load_sem.at[k])
        for k, (src, dst) in enumerate(
            ((gate_hbm, gate_v), (up_hbm, up_v), (weight_hbm, weight_v))
        )
    ]
    for load in loads:
        load.start()

    barrier = pltpu.get_barrier_semaphore()
    for k in range(1, narrow):
        pl.semaphore_signal(
            barrier, inc=1, device_id={"narrow": lax.rem(me_n + k, narrow)}, device_id_type=MESH
        )
    for k in range(1, wide):
        pl.semaphore_signal(
            barrier, inc=1, device_id={"wide": lax.rem(me_w + k, wide)}, device_id_type=MESH
        )
    for peer in (right, left):
        pl.semaphore_signal(barrier, inc=1, device_id={"dp": peer}, device_id_type=MESH)

    routes_pad[...] = jnp.full((top, LANES), -1, jnp.int32)
    gates_pad[...] = jnp.zeros((top, LANES), F32)
    routes_pad[:, 0:tok] = routes_ref[...]
    gates_pad[:, 0:tok] = gates_ref[...].astype(F32)
    square = (LANES, LANES)
    expert_row = iota(square, 0)
    hits = jnp.zeros(square, F32)
    gate_at = jnp.zeros(square, F32)
    for k in range(top):
        same = routes_pad[k : k + 1, :] == expert_row
        hits = hits + jnp.where(same, 1.0, 0.0)
        gate_at = gate_at + jnp.where(same, gates_pad[k : k + 1, :], 0.0)
    earlier = jnp.where(iota(square, 0) < iota(square, 1), 1.0, 0.0).astype(BF16)
    before = jnp.dot(hits.astype(BF16), earlier, preferred_element_type=F32)
    for k in range(top):
        same = routes_pad[k : k + 1, :] == expert_row
        place[k : k + 1, :] = jnp.sum(jnp.where(same, before, 0.0), axis=0, keepdims=True)
    unit = jnp.where(iota((tok, LANES), 0) == iota((tok, LANES), 1), 1.0, 0.0).astype(BF16)
    for p in range(2):
        held = jnp.where(before == float(p), gate_at, 0.0).astype(BF16)
        table[:, p * LANES : (p + 1) * LANES] = lax.dot_general(
            unit, held, NT, preferred_element_type=F32
        ).astype(BF16)

    whole(tokens, token_sem)
    pl.semaphore_wait(barrier, (narrow - 1) + (wide - 1) + 2)

    def to_narrow(src, dst, send, recv):
        for k in range(1, narrow):
            pltpu.make_async_remote_copy(
                src_ref=src, dst_ref=dst.at[me_n], send_sem=send, recv_sem=recv,
                device_id={"narrow": lax.rem(me_n + k, narrow)}, device_id_type=MESH,
            ).start()
        pltpu.make_async_copy(src, dst.at[me_n], recv).start()

    def to_wide(src, dst, send, recv):
        for k in range(1, wide):
            peer = lax.rem(me_w + k, wide)
            pltpu.make_async_remote_copy(
                src_ref=src.at[peer], dst_ref=dst.at[me_w], send_sem=send, recv_sem=recv,
                device_id={"wide": peer}, device_id_type=MESH,
            ).start()
        pltpu.make_async_copy(src.at[me_w], dst.at[me_w], recv).start()

    def spread(step):
        to_narrow(tokens.at[step], gathered.at[step], token_send, token_recv.at[step])

    to_narrow(table, tables, table_send, table_recv)
    for step in range(AHEAD + 1):
        spread(step)

    for load in loads[:2]:
        load.wait()

    @pl.loop(0, blocks)
    def _(b):
        col = pl.ds(pl.multiple_of(b * LANES, LANES), LANES)
        gate = gate_v[:, col].astype(F32)
        up = up_v[:, col].astype(F32)
        sig = jax.nn.sigmoid(gate)
        silu = gate * sig
        hidden[:, col] = (silu * up).astype(BF16)
        factor_a[:, col] = up * sig * (1.0 + gate * (1.0 - sig))
        factor_b[:, col] = silu

    whole(tables, table_recv)
    pair = (slots, 2 * LANES)
    slot_row, entry = iota(pair, 0), iota(pair, 1)
    wanted = ((slot_row >> 4) * narrow + me_n) + (slot_row & 1) * LANES
    pick = jnp.where(entry == wanted, 1.0, 0.0).astype(BF16)
    full = lax.dot_general(
        pick, tables[...].reshape(narrow * tok, 2 * LANES), NT, preferred_element_type=F32
    )
    shape = (slots, narrow * tok)
    mine = ((iota(shape, 0) >> 1) & (narrow - 1)) == (iota(shape, 1) >> 4)
    gate_of = jnp.where(mine, full, 0.0)
    choose[...] = jnp.where(gate_of > 0.0, 1.0, 0.0).astype(BF16)
    gate_sum = jnp.sum(gate_of, axis=1, keepdims=True)
    gate_send[...] = (
        jnp.broadcast_to(gate_sum, (slots, LANES)).astype(BF16).reshape(wide, 2 * narrow, LANES)
    )
    to_wide(gate_send, gate_rows, gates_send, gates_recv)

    def forward(step):
        whole(gathered.at[step], token_recv.at[step])
        for half in range(2):
            held = gathered[step, :, half * tok : (half + 1) * tok, :].reshape(narrow * tok, LANES)
            picked = jnp.dot(choose[...], held, preferred_element_type=F32).astype(BF16)
            rows_out[step, :, half * tok : (half + 1) * tok, :] = picked.reshape(
                wide, 2 * narrow, LANES
            )
        to_wide(rows_out.at[step], rows_in.at[step], rows_send, rows_recv.at[step])

    forward(0)
    spread(AHEAD + 1)
    forward(1)
    spread(AHEAD + 2)

    whole(gate_rows, gates_recv)
    for b in range(blocks):
        col = slice(b * LANES, (b + 1) * LANES)
        gate = gate_rows[...].reshape(slots, LANES).astype(F32)
        scaled = (gate * hidden[:, col].astype(F32)).astype(BF16).astype(F32)
        scaled_t[b * LANES : (b + 1) * LANES, :] = scaled.T.astype(BF16)
    back_prop[...] = jnp.zeros_like(back_prop)

    forward(2)
    spread(AHEAD + 3)

    def rows(step, half):
        return rows_in[step, :, half * tok : (half + 1) * tok, :].reshape(slots, LANES)

    def arrive(step):
        whole(rows_in.at[step], rows_recv.at[step])

    def partial_of(step):
        for half in range(2):
            part_sum[half] = jnp.dot(scaled_t[...], rows(step, half), preferred_element_type=F32)

    def copy_of(step, half, sub, peer):
        at = pl.ds(sub * sub_rows, sub_rows)
        return pltpu.make_async_remote_copy(
            src_ref=part_out.at[step, half, at],
            dst_ref=part_in.at[step, half, at],
            send_sem=part_send,
            recv_sem=part_recv.at[step, half, sub],
            device_id={"dp": peer},
            device_id_type=MESH,
        )

    def ring(step, first):
        partial_of(step)
        for sub in range(SUBS):
            at = slice(sub * sub_rows, (sub + 1) * sub_rows)
            for half, peer in enumerate((right, left)):
                value = part_sum[half, at, :]
                if not first:
                    copy_of(step - 1, half, sub, peer).wait_recv()
                    value = value + part_in[step - 1, half, at, :].astype(F32)
                part_out[step, half, at, :] = value.astype(BF16)
                copy_of(step, half, sub, peer).start()

    def back(step):
        total = back_prop[...]
        for half, col in enumerate(columns(step)):
            total = total + lax.dot_general(
                rows(step, half), weight_v[:, pl.ds(col, LANES)], NT, preferred_element_type=F32
            )
        back_prop[...] = total

    arrive(0)
    ring(0, True)
    forward(3)
    spread(AHEAD + 4)
    loads[2].wait()
    back(0)

    @pl.loop(1, dp - AHEAD)
    def _(step):
        arrive(step)
        ring(step, False)
        forward(step + AHEAD)
        back(step)

    arrive(dp - 3)
    ring(dp - 3, False)
    back(dp - 3)
    for step in (dp - 2, dp - 1):
        arrive(step)
        back(step)

    dots = jnp.zeros((slots, LANES), F32)
    for b in range(blocks):
        col = slice(b * LANES, (b + 1) * LANES)
        bp = back_prop[:, col]
        gate = gate_rows[...].reshape(slots, LANES).astype(F32)
        carried = gate * bp
        dots = dots + hidden[:, col].astype(F32) * bp
        gate_v[:, col] = (carried * factor_a[:, col]).astype(BF16)
        up_v[:, col] = (carried * factor_b[:, col]).astype(BF16)
    sums = jnp.sum(dots, axis=1, keepdims=True)
    slot_out[...] = jnp.broadcast_to(sums, (slots, LANES)).reshape(wide, 2 * narrow, LANES)
    to_wide(slot_out, slot_in, slot_send, slot_recv)
    stores = [
        pltpu.make_async_copy(gate_v, dgate_out, store_sem.at[0]),
        pltpu.make_async_copy(up_v, dup_out, store_sem.at[1]),
    ]
    for store in stores:
        store.start()

    ring(dp - 2, False)

    whole(slot_in, slot_recv)
    flat = (2 * narrow, LANES)
    packed = jnp.zeros(flat, F32)
    for k in range(wide):
        packed = packed + jnp.where(iota(flat, 1) == me_n * wide + k, slot_in[k], 0.0)
    pack_out[...] = packed
    to_narrow(pack_out, pack_in, pack_send, pack_recv)

    partial_of(dp - 1)
    for sub in range(SUBS):
        at = slice(sub * sub_rows, (sub + 1) * sub_rows)
        for half, peer in enumerate((right, left)):
            copy_of(dp - 2, half, sub, peer).wait_recv()
            value = part_sum[half, at, :] + part_in[dp - 2, half, at, :].astype(F32)
            down_v[at, half * LANES : (half + 1) * LANES] = value.astype(BF16)
    last = pltpu.make_async_copy(down_v, down_out, store_sem.at[2])
    last.start()

    whole(pack_in, pack_recv)
    back_rows = jnp.sum(pack_in[...], axis=0)
    for k in range(top):
        named = routes_pad[k : k + 1, :]
        lane = (named & (narrow - 1)) * wide + (named >> 3)
        one = jnp.where(lane == iota(square, 0), 1.0, 0.0)
        got = jnp.dot(
            back_rows, one, precision=lax.Precision.HIGHEST, preferred_element_type=F32
        )
        row = 2 * me_n + place[k : k + 1, :].astype(jnp.int32)
        value = jnp.sum(jnp.where(iota(flat, 0) == row, got, 0.0), axis=0, keepdims=True)
        droute_ref[k : k + 1, :] = value[:, 0:tok]

    for store in stores:
        store.wait()
    last.wait()
    peers_n, peers_w = pl.ds(0, narrow - 1), pl.ds(0, wide - 1)
    for step in range(dp):
        whole(gathered.at[step, peers_n], token_send)
        whole(rows_in.at[step, peers_w], rows_send)
    whole(tables.at[peers_n], table_send)
    whole(gate_rows.at[peers_w], gates_send)
    whole(slot_in.at[peers_w], slot_send)
    whole(pack_in.at[peers_n], pack_send)
    whole(part_in, part_send)


def shards(out_grad, routes, gates, pre_gate, pre_up, down_weight):
    dp, wide, narrow = (lax.axis_size(a) for a in ("dp", "wide", "narrow"))
    tok, feat = out_grad.shape
    top = routes.shape[1]
    slots, hid = pre_gate.shape[2:]
    dims = (dp, wide, narrow, tok, top, feat, hid, slots)
    vmem, dma = pltpu.VMEM, pltpu.SemaphoreType.DMA
    any_spec = pl.BlockSpec(memory_space=pl.ANY)
    vmem_spec = pl.BlockSpec(memory_space=pltpu.VMEM)
    down, dgate, dup, droute = pl.pallas_call(
        functools.partial(kernel, dims),
        out_shape=(
            jax.ShapeDtypeStruct((hid, feat // dp), BF16),
            jax.ShapeDtypeStruct((slots, hid), BF16),
            jax.ShapeDtypeStruct((slots, hid), BF16),
            jax.ShapeDtypeStruct((top, tok), F32),
        ),
        in_specs=[any_spec, vmem_spec, vmem_spec, any_spec, any_spec, any_spec],
        out_specs=(any_spec, any_spec, any_spec, vmem_spec),
        scratch_shapes=[
            vmem((slots, hid), BF16),
            vmem((slots, hid), BF16),
            vmem((hid, feat), BF16),
            vmem((dp, 2 * tok, LANES), BF16),
            vmem((tok, 2 * LANES), BF16),
            vmem((top, LANES), jnp.int32),
            vmem((top, LANES), F32),
            vmem((top, LANES), F32),
            vmem((slots, hid), BF16),
            vmem((slots, hid), F32),
            vmem((slots, hid), F32),
            vmem((dp, narrow, 2 * tok, LANES), BF16),
            vmem((narrow, tok, 2 * LANES), BF16),
            vmem((slots, narrow * tok), BF16),
            vmem((dp, wide, 2 * tok, LANES), BF16),
            vmem((dp, wide, 2 * tok, LANES), BF16),
            vmem((wide, 2 * narrow, LANES), BF16),
            vmem((wide, 2 * narrow, LANES), BF16),
            vmem((hid, slots), BF16),
            vmem((slots, hid), F32),
            vmem((dp - 1, 2, hid, LANES), BF16),
            vmem((dp - 1, 2, hid, LANES), BF16),
            vmem((2, hid, LANES), F32),
            vmem((hid, 2 * LANES), BF16),
            vmem((wide, 2 * narrow, LANES), F32),
            vmem((wide, 2 * narrow, LANES), F32),
            vmem((2 * narrow, LANES), F32),
            vmem((narrow, 2 * narrow, LANES), F32),
            dma((3,)),
            dma,
            dma,
            dma((dp,)),
            dma,
            dma,
            dma,
            dma((dp,)),
            dma,
            dma,
            dma,
            dma((dp - 1, 2, SUBS)),
            dma,
            dma,
            dma,
            dma,
            dma((3,)),
        ],
        compiler_params=pltpu.CompilerParams(collective_id=0, has_side_effects=True),
        name="routed_backward",
    )(out_grad, routes.T, gates.T, pre_gate[0, 0], pre_up[0, 0], down_weight[0])
    return down[None], dgate[None, None], dup[None, None], droute.T


def solution(mesh):
    placed = (
        P(("dp", "wide", "narrow"), None),
        P(("dp", "wide", "narrow"), None),
        P(("dp", "wide", "narrow"), None),
        P("dp", ("wide", "narrow"), None, None),
        P("dp", ("wide", "narrow"), None, None),
        P(("wide", "narrow"), None, None),
    )
    return jax.shard_map(
        shards,
        mesh=mesh,
        in_specs=placed,
        out_specs=(
            P(("wide", "narrow"), None, "dp"),
            P("dp", ("wide", "narrow"), None, None),
            P("dp", ("wide", "narrow"), None, None),
            P(("dp", "wide", "narrow"), None),
        ),
        check_vma=False,
    )
```

time: 208 us -> 83.4 us (0.40)
  waiting for transfers between devices: 115 us -> 0 us
  Pallas kernels: 0 us -> 75.9 us
  starting transfers between devices: 42 us -> 0 us
  local copies, waits for them, and re-layouts: 20.6 us -> 6.57 us
  between operations: 14.1 us -> 0.64 us
  matrix products: 11.1 us -> 0 us
  other arithmetic: 4.07 us -> 0 us
    pallas_call x0 -> x1, Pallas kernels: none -> 75.9 us  [shards(): pl.pallas_call(functools.partial(kernel, dims), out_shape=(jax.ShapeDtype...]
    all_to_all x6 -> x0, waiting for transfers between devices: 72.9 us -> none  [the longest x1 27.4 us: shards(): lax.all_to_all(outgoing, 'wide', split_axis=0, concat_axis=0, tiled=True)]
    reduce_scatter x1 -> x0, waiting for transfers between devices: 42.6 us -> none  [shards(): lax.psum_scatter(partial_value, 'dp', scatter_dimension=1, tiled=True)]
    all_to_all x6 -> x0, starting transfers between devices: 41.9 us -> none  [the longest x1 17.4 us: shards(): lax.all_to_all(gate_out, 'wide', split_axis=0, concat_axis=0, tiled=True)]
    dot_general x3 -> x0, matrix products: 11.1 us -> none  [the longest x1 5.14 us: shards(): lax.dot_general(scaled, routed_rows, (((0,), (0,)), ((), ())), preferred_...]
    all_to_all x5 -> x0, local copies, waits for them, and re-layouts: 7.81 us -> none  [the longest x1 3.23 us: shards(): lax.all_to_all(lax.all_to_all(outgoing, 'wide', split_axis=0, concat_axis...]
    reshape x6 -> x0, local copies, waits for them, and re-layouts: 6.45 us -> none  [the longest x1 2.54 us: shards(): outgoing.reshape(wide_count, narrow_count, capacity, outgoing.shape[1])]
    unnamed x8 -> x4, local copies, waits for them, and re-layouts: 1.59 us -> 6.57 us
  transfers between devices with their start and end apart: 7 -> 0, of which waited for: 7 -> 0; matrix products, arithmetic and copies ran while one was open for 10% -> 0% of each run, Pallas kernels for 0% -> 0%
where the time goes in v1:
time: 83.4 us; the launch traced here: 83.1 us
  Pallas kernels  75.9 us (91%)
  local copies, waits for them, and re-layouts  6.57 us (8%)
    pallas_call x1, Pallas kernels, shards(): pl.pallas_call(functools.partial(kernel, dims), out_shape=(jax.ShapeDtype...  75.9 us
    unnamed x4, local copies, waits for them, and re-layouts  6.57 us

profile of v1, /device:TPU:1, one launch (start us, length us, event | category | flops | bytes accessed | tf_op | source)
XLA Modules:
  0.0 83.1 jit_solution(12474264212691658803)
XLA Ops:
  0.6 75.9 %routed_backward.1 = (bf16[768,256]{1,0:T(8,128)(2,1)}, bf16[256,768]{1,0:T(8,128)(2,1)}, bf16[256,768]{1,0:T(8,128)(2,1)}, f32[8,16]{1,0:T(8,128)}) custom-call(bf16[16,2048]{1,0:T(8,128)(2,1)} %grads_hbm.1, s32[8,16]{1,0:T(8,128)} %bitcast.16, bf16[8,16]{1,0:T(8,128)(2,1)} %bitcast.17, bf16[256,768]{1,0:T(8,128)(2,1)} %bitcast.10, ...), custom_call_target="tpu_custom_call" | custom-call | tf_op jit(solution)/shard_map/routed_backward/pallas_call | solution.py:323
  76.5 1.8 %copy.14 = bf16[1,768,256]{2,1,0:T(8,128)(2,1)} copy(bf16[1,768,256]{2,1,0:T(8,128)(2,1)} %bitcast.14) | data formatting | bytes 786432
  78.3 1.8 %copy.15 = bf16[1,1,256,768]{3,2,1,0:T(8,128)(2,1)} copy(bf16[1,1,256,768]{3,2,1,0:T(8,128)(2,1)} %bitcast.13) | data formatting | bytes 786432
  80.1 1.8 %copy.16 = bf16[1,1,256,768]{3,2,1,0:T(8,128)(2,1)} copy(bf16[1,1,256,768]{3,2,1,0:T(8,128)(2,1)} %bitcast.12) | data formatting | bytes 786432
  81.8 1.3 %copy.17 = f32[16,8]{0,1:T(8,128)} copy(f32[16,8]{0,1:T(8,128)} %bitcast.15) | data formatting | bytes 1024

commit v2 on v1

v2 whole, which is shorter than its diff:
```python
import functools

import jax
import jax.numpy as jnp
from jax import lax
from jax.experimental import pallas as pl
from jax.experimental.pallas import tpu as pltpu
from jax.sharding import PartitionSpec as P

MESH = pl.DeviceIdType.MESH
F32 = jnp.float32
BF16 = jnp.bfloat16
LANES = 128
SUBS = 4
AHEAD = 4
NT = (((1,), (1,)), ((), ()))


def iota(shape, dim):
    return lax.broadcasted_iota(jnp.int32, shape, dim)


def kernel(
    dims,
    grads_hbm, routes_hbm, gates_hbm, gate_hbm, up_hbm, weight_hbm,
    down_out, dgate_out, dup_out, droute_out,
    routes_v, gates_v, gate_v, up_v, weight_v, tokens, table, routes_pad, gates_pad, ranks, place,
    hidden, factor_a, factor_b, gathered, tables, choose,
    rows_out, rows_in, gate_send, gate_recv, gate_rows, scaled_t, back_prop,
    part_out, part_in, part_sum, down_v, droute_v, slot_out, slot_in, pack_out, pack_in,
    small_sem, load_sem, token_sem, token_send, token_recv, table_send, table_recv,
    rows_send, rows_recv, gates_send, gates_recv, part_send, part_recv,
    slot_send, slot_recv, pack_send, pack_recv, store_sem,
):
    dp, wide, narrow, tok, top, feat, hid, slots = dims
    me_x, me_w, me_n = (lax.axis_index(a) for a in ("dp", "wide", "narrow"))
    right, left = lax.rem(me_x + 1, dp), lax.rem(me_x + dp - 1, dp)
    sub_rows = hid // SUBS
    blocks = hid // LANES

    def columns(step):
        first = lax.rem(me_x + (2 * dp - 1) - step, dp) * (2 * LANES)
        second = lax.rem(me_x + 1 + step, dp) * (2 * LANES) + LANES
        return pl.multiple_of(first, LANES), pl.multiple_of(second, LANES)

    def whole(ref, sem):
        pltpu.make_async_copy(ref, ref, sem).wait()

    near = sorted(range(1, narrow), key=lambda k: -min(k, narrow - k))
    far = sorted(range(1, wide), key=lambda k: -min(k, wide - k))
    barrier = pltpu.get_barrier_semaphore()
    for k in near:
        pl.semaphore_signal(
            barrier, inc=1, device_id={"narrow": lax.rem(me_n + k, narrow)}, device_id_type=MESH
        )
    for k in far:
        pl.semaphore_signal(
            barrier, inc=1, device_id={"wide": lax.rem(me_w + k, wide)}, device_id_type=MESH
        )
    for peer in (right, left):
        pl.semaphore_signal(barrier, inc=1, device_id={"dp": peer}, device_id_type=MESH)

    small = [
        pltpu.make_async_copy(src, dst, small_sem.at[k])
        for k, (src, dst) in enumerate(((routes_hbm, routes_v), (gates_hbm, gates_v)))
    ]
    for load in small:
        load.start()
    for step in range(dp):
        for half, col in enumerate(columns(step)):
            pltpu.make_async_copy(
                grads_hbm.at[:, pl.ds(col, LANES)],
                tokens.at[step, pl.ds(half * tok, tok)],
                token_sem,
            ).start()
    loads = [
        pltpu.make_async_copy(src, dst, load_sem.at[k])
        for k, (src, dst) in enumerate(
            ((gate_hbm, gate_v), (up_hbm, up_v), (weight_hbm, weight_v))
        )
    ]

    routes_pad[...] = jnp.full((top, LANES), -1, jnp.int32)
    gates_pad[...] = jnp.zeros((top, LANES), F32)
    for load in small:
        load.wait()
    routes_pad[:, 0:tok] = routes_v[...]
    gates_pad[:, 0:tok] = gates_v[...].astype(F32)
    square = (LANES, LANES)
    expert_row = iota(square, 0)
    hits = jnp.zeros(square, F32)
    gate_at = jnp.zeros(square, F32)
    for k in range(top):
        same = routes_pad[k : k + 1, :] == expert_row
        hits = jnp.where(same, 1.0, hits)
        gate_at = jnp.where(same, gates_pad[k : k + 1, :], gate_at)
    earlier = jnp.where(iota(square, 0) < iota(square, 1), 1.0, 0.0).astype(BF16)
    before = jnp.dot(hits.astype(BF16), earlier, preferred_element_type=F32)
    ranks[...] = before
    unit = jnp.where(iota((tok, LANES), 0) == iota((tok, LANES), 1), 1.0, 0.0).astype(BF16)
    held = jnp.where(before == 0.0, gate_at, jnp.where(before == 1.0, -gate_at, 0.0)).astype(BF16)
    table[...] = lax.dot_general(unit, held, NT, preferred_element_type=F32).astype(BF16)

    pl.semaphore_wait(barrier, (narrow - 1) + (wide - 1) + 2)

    def to_narrow(src, dst, send, recv):
        for k in near:
            pltpu.make_async_remote_copy(
                src_ref=src, dst_ref=dst.at[me_n], send_sem=send, recv_sem=recv,
                device_id={"narrow": lax.rem(me_n + k, narrow)}, device_id_type=MESH,
            ).start()
        pltpu.make_async_copy(src, dst.at[me_n], recv).start()

    def to_wide(src, dst, send, recv):
        for k in far:
            peer = lax.rem(me_w + k, wide)
            pltpu.make_async_remote_copy(
                src_ref=src.at[peer], dst_ref=dst.at[me_w], send_sem=send, recv_sem=recv,
                device_id={"wide": peer}, device_id_type=MESH,
            ).start()
        pltpu.make_async_copy(src.at[me_w], dst.at[me_w], recv).start()

    def spread(step):
        to_narrow(tokens.at[step], gathered.at[step], token_send, token_recv.at[step])

    to_narrow(table, tables, table_send, table_recv)
    whole(tokens, token_sem)
    for step in range(AHEAD):
        spread(step)
    for load in loads:
        load.start()

    for k in range(top):
        same = routes_pad[k : k + 1, :] == expert_row
        place[k : k + 1, :] = jnp.sum(jnp.where(same, ranks[...], 0.0), axis=0, keepdims=True)
    for load in loads[:2]:
        load.wait()

    @pl.loop(0, blocks)
    def _(b):
        col = pl.ds(pl.multiple_of(b * LANES, LANES), LANES)
        gate = gate_v[:, col].astype(F32)
        up = up_v[:, col].astype(F32)
        sig = jax.nn.sigmoid(gate)
        silu = gate * sig
        hidden[:, col] = (silu * up).astype(BF16)
        factor_a[:, col] = up * sig * (1.0 + gate * (1.0 - sig))
        factor_b[:, col] = silu

    whole(tables, table_recv)
    shape = (slots, narrow * tok)
    slot_row, entry = iota(shape, 0), iota(shape, 1)
    pick = jnp.where(entry == (slot_row >> 4) * narrow + me_n, 1.0, 0.0).astype(BF16)
    full = lax.dot_general(
        pick, tables[...].reshape(narrow * tok, LANES), NT, preferred_element_type=F32
    )
    mine = ((slot_row >> 1) & (narrow - 1)) == (entry >> 4)
    signed = jnp.where((slot_row & 1) == 0, full, -full)
    gate_of = jnp.where(mine, jnp.maximum(signed, 0.0), 0.0)
    choose[...] = jnp.where(gate_of > 0.0, 1.0, 0.0).astype(BF16)

    cube = (wide, 2 * narrow, LANES)
    diagonal = iota(cube, 1) == iota(cube, 2)

    def to_lanes(column):
        spread_out = jnp.broadcast_to(column, (slots, LANES)).reshape(cube)
        return jnp.sum(jnp.where(diagonal, spread_out, 0.0), axis=1, keepdims=True)

    def to_rows(lanes):
        spread_out = jnp.where(diagonal, jnp.broadcast_to(lanes, cube), 0.0)
        return jnp.broadcast_to(jnp.sum(spread_out, axis=2, keepdims=True), cube)

    gate_send[...] = to_lanes(jnp.sum(gate_of, axis=1, keepdims=True))
    to_wide(gate_send, gate_recv, gates_send, gates_recv)

    def forward(step):
        whole(gathered.at[step], token_recv.at[step])
        for half in range(2):
            held = gathered[step, :, half * tok : (half + 1) * tok, :].reshape(narrow * tok, LANES)
            picked = jnp.dot(choose[...], held, preferred_element_type=F32).astype(BF16)
            rows_out[step, :, half * tok : (half + 1) * tok, :] = picked.reshape(
                wide, 2 * narrow, LANES
            )
        to_wide(rows_out.at[step], rows_in.at[step], rows_send, rows_recv.at[step])

    forward(0)
    spread(AHEAD)
    forward(1)
    spread(AHEAD + 1)

    whole(gate_recv, gates_recv)
    gate_rows[...] = to_rows(gate_recv[...]).reshape(slots, LANES)
    for b in range(blocks):
        col = slice(b * LANES, (b + 1) * LANES)
        scaled = (gate_rows[...] * hidden[:, col].astype(F32)).astype(BF16).astype(F32)
        scaled_t[b * LANES : (b + 1) * LANES, :] = scaled.T.astype(BF16)
    back_prop[...] = jnp.zeros_like(back_prop)

    forward(2)
    spread(AHEAD + 2)
    forward(3)
    spread(AHEAD + 3)

    def rows(step, half):
        return rows_in[step, :, half * tok : (half + 1) * tok, :].reshape(slots, LANES)

    def arrive(step):
        whole(rows_in.at[step], rows_recv.at[step])

    def partial_of(step):
        for half in range(2):
            part_sum[half] = jnp.dot(scaled_t[...], rows(step, half), preferred_element_type=F32)

    def copy_of(step, half, sub, peer):
        at = pl.ds(sub * sub_rows, sub_rows)
        return pltpu.make_async_remote_copy(
            src_ref=part_out.at[step, half, at],
            dst_ref=part_in.at[step, half, at],
            send_sem=part_send,
            recv_sem=part_recv.at[step, half, sub],
            device_id={"dp": peer},
            device_id_type=MESH,
        )

    def ring(step, first, between=None):
        partial_of(step)
        for sub in range(SUBS):
            if sub == SUBS // 2 and between is not None:
                between()
            at = slice(sub * sub_rows, (sub + 1) * sub_rows)
            for half, peer in enumerate((right, left)):
                value = part_sum[half, at, :]
                if not first:
                    copy_of(step - 1, half, sub, peer).wait_recv()
                    value = value + part_in[step - 1, half, at, :].astype(F32)
                part_out[step, half, at, :] = value.astype(BF16)
                copy_of(step, half, sub, peer).start()

    def back(step):
        total = back_prop[...]
        for half, col in enumerate(columns(step)):
            total = total + lax.dot_general(
                rows(step, half), weight_v[:, pl.ds(col, LANES)], NT, preferred_element_type=F32
            )
        back_prop[...] = total

    arrive(0)
    ring(0, True)
    forward(AHEAD)
    loads[2].wait()
    back(0)

    @pl.loop(1, dp - AHEAD)
    def _(step):
        arrive(step)
        ring(step, False)
        forward(step + AHEAD)
        back(step)

    @pl.loop(dp - AHEAD, dp - 3)
    def _(step):
        arrive(step)
        ring(step, False)
        back(step)

    stores = [
        pltpu.make_async_copy(gate_v, dgate_out, store_sem.at[0]),
        pltpu.make_async_copy(up_v, dup_out, store_sem.at[1]),
    ]

    def finish():
        back(dp - 3)
        for step in (dp - 2, dp - 1):
            arrive(step)
            back(step)
        dots = jnp.zeros((slots, LANES), F32)
        for b in range(blocks):
            col = slice(b * LANES, (b + 1) * LANES)
            dots = dots + hidden[:, col].astype(F32) * back_prop[:, col]
        slot_out[...] = to_lanes(jnp.sum(dots, axis=1, keepdims=True))
        to_wide(slot_out, slot_in, slot_send, slot_recv)

    arrive(dp - 3)
    ring(dp - 3, False, finish)
    for b in range(blocks):
        col = slice(b * LANES, (b + 1) * LANES)
        carried = gate_rows[...] * back_prop[:, col]
        gate_v[:, col] = (carried * factor_a[:, col]).astype(BF16)
        up_v[:, col] = (carried * factor_b[:, col]).astype(BF16)
    for store in stores:
        store.start()
    ring(dp - 2, False)

    whole(slot_in, slot_recv)
    here = iota(cube, 2) == me_n * wide + iota(cube, 0)
    packed = jnp.sum(jnp.where(here, to_rows(slot_in[...]), 0.0), axis=0)
    for k in range(2 * narrow):
        pack_out[k // 2, k % 2 : k % 2 + 1, :] = packed[k : k + 1, :]
    for k in near:
        peer = lax.rem(me_n + k, narrow)
        pltpu.make_async_remote_copy(
            src_ref=pack_out.at[peer], dst_ref=pack_in.at[me_n],
            send_sem=pack_send, recv_sem=pack_recv,
            device_id={"narrow": peer}, device_id_type=MESH,
        ).start()
    pltpu.make_async_copy(pack_out.at[me_n], pack_in.at[me_n], pack_recv).start()

    partial_of(dp - 1)
    for sub in range(SUBS):
        at = slice(sub * sub_rows, (sub + 1) * sub_rows)
        for half, peer in enumerate((right, left)):
            copy_of(dp - 2, half, sub, peer).wait_recv()
            value = part_sum[half, at, :] + part_in[dp - 2, half, at, :].astype(F32)
            down_v[at, half * LANES : (half + 1) * LANES] = value.astype(BF16)
    last = pltpu.make_async_copy(down_v, down_out, store_sem.at[2])
    last.start()

    whole(pack_in, pack_recv)
    back_rows = jnp.sum(pack_in[...], axis=0)
    for k in range(top):
        named = routes_pad[k : k + 1, :]
        lane = (named & (narrow - 1)) * wide + (named >> 3)
        one = jnp.where(lane == expert_row, 1.0, 0.0)
        got = jnp.dot(
            back_rows, one, precision=lax.Precision.HIGHEST, preferred_element_type=F32
        )
        value = jnp.where(place[k : k + 1, :] == 0.0, got[0:1, :], got[1:2, :])
        droute_v[k : k + 1, :] = value[:, 0:tok]
    routed = pltpu.make_async_copy(droute_v, droute_out, store_sem.at[3])
    routed.start()

    for store in stores:
        store.wait()
    last.wait()
    routed.wait()
    peers_n, peers_w = pl.ds(0, narrow - 1), pl.ds(0, wide - 1)
    for step in range(dp):
        whole(gathered.at[step, peers_n], token_send)
        whole(rows_in.at[step, peers_w], rows_send)
    whole(tables.at[peers_n], table_send)
    whole(gate_recv.at[peers_w], gates_send)
    whole(slot_in.at[peers_w], slot_send)
    whole(pack_in.at[peers_n], pack_send)
    whole(part_in, part_send)


def hand_on(*refs):
    sources, targets, held = refs[0:4], refs[4:8], refs[8:12]
    taken, given = refs[12:]
    reads = [pltpu.make_async_copy(a, b, taken.at[k]) for k, (a, b) in enumerate(zip(sources, held))]
    writes = [pltpu.make_async_copy(a, b, given.at[k]) for k, (a, b) in enumerate(zip(held, targets))]
    for read in reads:
        read.start()
    for read, write in zip(reads, writes):
        read.wait()
        write.start()
    for write in writes:
        write.wait()


def shards(out_grad, routes, gates, pre_gate, pre_up, down_weight):
    dp, wide, narrow = (lax.axis_size(a) for a in ("dp", "wide", "narrow"))
    tok, feat = out_grad.shape
    top = routes.shape[1]
    slots, hid = pre_gate.shape[2:]
    dims = (dp, wide, narrow, tok, top, feat, hid, slots)
    vmem, dma = pltpu.VMEM, pltpu.SemaphoreType.DMA
    any_spec = pl.BlockSpec(memory_space=pl.ANY)
    made = pl.pallas_call(
        functools.partial(kernel, dims),
        out_shape=(
            jax.ShapeDtypeStruct((hid, feat // dp), BF16),
            jax.ShapeDtypeStruct((slots, hid), BF16),
            jax.ShapeDtypeStruct((slots, hid), BF16),
            jax.ShapeDtypeStruct((top, tok), F32),
        ),
        in_specs=[any_spec] * 6,
        out_specs=(any_spec,) * 4,
        scratch_shapes=[
            vmem((top, tok), jnp.int32),
            vmem((top, tok), BF16),
            vmem((slots, hid), BF16),
            vmem((slots, hid), BF16),
            vmem((hid, feat), BF16),
            vmem((dp, 2 * tok, LANES), BF16),
            vmem((tok, LANES), BF16),
            vmem((top, LANES), jnp.int32),
            vmem((top, LANES), F32),
            vmem((LANES, LANES), F32),
            vmem((top, LANES), F32),
            vmem((slots, hid), BF16),
            vmem((slots, hid), F32),
            vmem((slots, hid), F32),
            vmem((dp, narrow, 2 * tok, LANES), BF16),
            vmem((narrow, tok, LANES), BF16),
            vmem((slots, narrow * tok), BF16),
            vmem((dp, wide, 2 * tok, LANES), BF16),
            vmem((dp, wide, 2 * tok, LANES), BF16),
            vmem((wide, 1, LANES), F32),
            vmem((wide, 1, LANES), F32),
            vmem((slots, LANES), F32),
            vmem((hid, slots), BF16),
            vmem((slots, hid), F32),
            vmem((dp - 1, 2, hid, LANES), BF16),
            vmem((dp - 1, 2, hid, LANES), BF16),
            vmem((2, hid, LANES), F32),
            vmem((hid, 2 * LANES), BF16),
            vmem((top, tok), F32),
            vmem((wide, 1, LANES), F32),
            vmem((wide, 1, LANES), F32),
            vmem((narrow, 2, LANES), F32),
            vmem((narrow, 2, LANES), F32),
            dma((2,)),
            dma((3,)),
            dma,
            dma,
            dma((dp,)),
            dma,
            dma,
            dma,
            dma((dp,)),
            dma,
            dma,
            dma,
            dma((dp - 1, 2, SUBS)),
            dma,
            dma,
            dma,
            dma,
            dma((4,)),
        ],
        compiler_params=pltpu.CompilerParams(collective_id=0, has_side_effects=True),
        name="routed_backward",
    )(out_grad, routes.T, gates.T, pre_gate[0, 0], pre_up[0, 0], down_weight[0])
    down, dgate, dup, droute = pl.pallas_call(
        hand_on,
        out_shape=tuple(jax.ShapeDtypeStruct(a.shape, a.dtype) for a in made),
        in_specs=[any_spec] * 4,
        out_specs=(any_spec,) * 4,
        scratch_shapes=[vmem(a.shape, a.dtype) for a in made] + [dma((4,)), dma((4,))],
        name="hand_on",
    )(*made)
    return down[None], dgate[None, None], dup[None, None], droute.T


def solution(mesh):
    placed = (
        P(("dp", "wide", "narrow"), None),
        P(("dp", "wide", "narrow"), None),
        P(("dp", "wide", "narrow"), None),
        P("dp", ("wide", "narrow"), None, None),
        P("dp", ("wide", "narrow"), None, None),
        P(("wide", "narrow"), None, None),
    )
    return jax.shard_map(
        shards,
        mesh=mesh,
        in_specs=placed,
        out_specs=(
            P(("wide", "narrow"), None, "dp"),
            P("dp", ("wide", "narrow"), None, None),
            P("dp", ("wide", "narrow"), None, None),
            P(("dp", "wide", "narrow"), None),
        ),
        check_vma=False,
    )
```

time: 83.4 us -> 71.4 us (0.86)
  local copies, waits for them, and re-layouts: 6.57 us -> 0 us
  Pallas kernels: 75.9 us -> 69.8 us
    pallas_call x1, Pallas kernels: 75.9 us -> 67.7 us  [shards(): pl.pallas_call(functools.partial(kernel, dims), out_shape=(jax.ShapeDtype...]
    unnamed x4 -> x0, local copies, waits for them, and re-layouts: 6.57 us -> none
    pallas_call x0 -> x1, Pallas kernels: none -> 2.07 us  [shards(): pl.pallas_call(hand_on, out_shape=tuple((jax.ShapeDtypeStruct(a.shape, a....]
where the time goes in v2:
time: 71.4 us; the launch traced here: 70.4 us
  Pallas kernels  69.8 us (98%)
    pallas_call x1, Pallas kernels, shards(): pl.pallas_call(functools.partial(kernel, dims), out_shape=(jax.ShapeDtype...  67.7 us
    pallas_call x1, Pallas kernels, shards(): pl.pallas_call(hand_on, out_shape=tuple((jax.ShapeDtypeStruct(a.shape, a....  2.07 us

profile of v2, /device:TPU:1, one launch (start us, length us, event | category | flops | bytes accessed | tf_op | source)
XLA Modules:
  0.0 70.4 jit_solution(5678710412111689214)
XLA Ops:
  0.6 67.7 %routed_backward.1 = (bf16[768,256]{1,0:T(8,128)(2,1)}, bf16[256,768]{1,0:T(8,128)(2,1)}, bf16[256,768]{1,0:T(8,128)(2,1)}, f32[8,16]{1,0:T(8,128)}) custom-call(bf16[16,2048]{1,0:T(8,128)(2,1)} %grads_hbm.1, s32[8,16]{1,0:T(8,128)} %bitcast.12, bf16[8,16]{1,0:T(8,128)(2,1)} %bitcast.13, bf16[256,768]{1,0:T(8,128)(2,1)} %bitcast.10, ...), custom_call_target="tpu_custom_call" | custom-call | tf_op jit(solution)/shard_map/routed_backward/pallas_call | solution.py:369
  68.3 2.1 %hand_on.1 = (bf16[768,256]{1,0:T(8,128)(2,1)}, bf16[256,768]{1,0:T(8,128)(2,1)}, bf16[256,768]{1,0:T(8,128)(2,1)}, f32[8,16]{1,0:T(8,128)}) custom-call(bf16[768,256]{1,0:T(8,128)(2,1)} %get-tuple-element.12.refs_0_, bf16[256,768]{1,0:T(8,128)(2,1)} %get-tuple-element.13.refs_1_, bf16[256,768]{1,0:T(8,128)(2,1)} %get-tuple-element.14.refs_2_, ...), custom_call_target="tpu_custom_call" | custom-call | tf_op jit(solution)/shard_map/hand_on/pallas_call | solution.py:435

commit v3 on v2

--- a/solution.py
+++ b/solution.py
@@ -12,7 +12,7 @@
 BF16 = jnp.bfloat16
 LANES = 128
 SUBS = 4
-AHEAD = 4
+FINISH = 1
 NT = (((1,), (1,)), ((), ()))
 
 
@@ -23,14 +23,14 @@
 def kernel(
     dims,
     grads_hbm, routes_hbm, gates_hbm, gate_hbm, up_hbm, weight_hbm,
-    down_out, dgate_out, dup_out, droute_out,
+    down_out, dgate_out, dup_out, pack_res, place_out,
     routes_v, gates_v, gate_v, up_v, weight_v, tokens, table, routes_pad, gates_pad, ranks, place,
     hidden, factor_a, factor_b, gathered, tables, choose,
     rows_out, rows_in, gate_send, gate_recv, gate_rows, scaled_t, back_prop,
-    part_out, part_in, part_sum, down_v, droute_v, slot_out, slot_in, pack_out, pack_in,
+    part_out, part_in, part_sum, down_v, slot_out, slot_in, pack_out, pack_in,
     small_sem, load_sem, token_sem, token_send, token_recv, table_send, table_recv,
     rows_send, rows_recv, gates_send, gates_recv, part_send, part_recv,
-    slot_send, slot_recv, pack_send, pack_recv, store_sem,
+    slot_send, slot_recv, pack_send, pack_recv, store_sem, down_sem,
 ):
     dp, wide, narrow, tok, top, feat, hid, slots = dims
     me_x, me_w, me_n = (lax.axis_index(a) for a in ("dp", "wide", "narrow"))
@@ -45,6 +45,13 @@
 
     def whole(ref, sem):
         pltpu.make_async_copy(ref, ref, sem).wait()
+
+    small = [
+        pltpu.make_async_copy(src, dst, small_sem.at[k])
+        for k, (src, dst) in enumerate(((routes_hbm, routes_v), (gates_hbm, gates_v)))
+    ]
+    for load in small:
+        load.start()
 
     near = sorted(range(1, narrow), key=lambda k: -min(k, narrow - k))
     far = sorted(range(1, wide), key=lambda k: -min(k, wide - k))
@@ -60,12 +67,6 @@
     for peer in (right, left):
         pl.semaphore_signal(barrier, inc=1, device_id={"dp": peer}, device_id_type=MESH)
 
-    small = [
-        pltpu.make_async_copy(src, dst, small_sem.at[k])
-        for k, (src, dst) in enumerate(((routes_hbm, routes_v), (gates_hbm, gates_v)))
-    ]
-    for load in small:
-        load.start()
     for step in range(dp):
         for half, col in enumerate(columns(step)):
             pltpu.make_async_copy(
@@ -125,27 +126,10 @@
 
     to_narrow(table, tables, table_send, table_recv)
     whole(tokens, token_sem)
-    for step in range(AHEAD):
+    for step in range(4):
         spread(step)
     for load in loads:
         load.start()
-
-    for k in range(top):
-        same = routes_pad[k : k + 1, :] == expert_row
-        place[k : k + 1, :] = jnp.sum(jnp.where(same, ranks[...], 0.0), axis=0, keepdims=True)
-    for load in loads[:2]:
-        load.wait()
-
-    @pl.loop(0, blocks)
-    def _(b):
-        col = pl.ds(pl.multiple_of(b * LANES, LANES), LANES)
-        gate = gate_v[:, col].astype(F32)
-        up = up_v[:, col].astype(F32)
-        sig = jax.nn.sigmoid(gate)
-        silu = gate * sig
-        hidden[:, col] = (silu * up).astype(BF16)
-        factor_a[:, col] = up * sig * (1.0 + gate * (1.0 - sig))
-        factor_b[:, col] = silu
 
     whole(tables, table_recv)
     shape = (slots, narrow * tok)
@@ -184,9 +168,29 @@
         to_wide(rows_out.at[step], rows_in.at[step], rows_send, rows_recv.at[step])
 
     forward(0)
-    spread(AHEAD)
+    spread(4)
+    spread(5)
+
+    for k in range(top):
+        same = routes_pad[k : k + 1, :] == expert_row
+        place[k : k + 1, :] = jnp.sum(jnp.where(same, ranks[...], 0.0), axis=0, keepdims=True)
+    for load in loads[:2]:
+        load.wait()
+
+    @pl.loop(0, blocks)
+    def _(b):
+        col = pl.ds(pl.multiple_of(b * LANES, LANES), LANES)
+        gate = gate_v[:, col].astype(F32)
+        up = up_v[:, col].astype(F32)
+        sig = jax.nn.sigmoid(gate)
+        silu = gate * sig
+        hidden[:, col] = (silu * up).astype(BF16)
+        factor_a[:, col] = up * sig * (1.0 + gate * (1.0 - sig))
+        factor_b[:, col] = silu
+
     forward(1)
-    spread(AHEAD + 1)
+    spread(6)
+    spread(7)
 
     whole(gate_recv, gates_recv)
     gate_rows[...] = to_rows(gate_recv[...]).reshape(slots, LANES)
@@ -195,11 +199,6 @@
         scaled = (gate_rows[...] * hidden[:, col].astype(F32)).astype(BF16).astype(F32)
         scaled_t[b * LANES : (b + 1) * LANES, :] = scaled.T.astype(BF16)
     back_prop[...] = jnp.zeros_like(back_prop)
-
-    forward(2)
-    spread(AHEAD + 2)
-    forward(3)
-    spread(AHEAD + 3)
 
     def rows(step, half):
         return rows_in[step, :, half * tok : (half + 1) * tok, :].reshape(slots, LANES)
@@ -222,10 +221,10 @@
             device_id_type=MESH,
         )
 
-    def ring(step, first, between=None):
+    def ring(step, first, between=None, when=0):
         partial_of(step)
         for sub in range(SUBS):
-            if sub == SUBS // 2 and between is not None:
+            if sub == when and between is not None:
                 between()
             at = slice(sub * sub_rows, (sub + 1) * sub_rows)
             for half, peer in enumerate((right, left)):
@@ -245,19 +244,20 @@
         back_prop[...] = total
 
     arrive(0)
+    forward(2)
     ring(0, True)
-    forward(AHEAD)
+    pl.loop(3, 5)(forward)
     loads[2].wait()
     back(0)
 
-    @pl.loop(1, dp - AHEAD)
+    @pl.loop(1, 3)
     def _(step):
         arrive(step)
         ring(step, False)
-        forward(step + AHEAD)
+        pl.loop(2 * step + 3, jnp.minimum(2 * step + 5, dp))(forward)
         back(step)
 
-    @pl.loop(dp - AHEAD, dp - 3)
+    @pl.loop(3, dp - 3)
     def _(step):
         arrive(step)
         ring(step, False)
@@ -281,7 +281,7 @@
         to_wide(slot_out, slot_in, slot_send, slot_recv)
 
     arrive(dp - 3)
-    ring(dp - 3, False, finish)
+    ring(dp - 3, False, finish, FINISH)
     for b in range(blocks):
         col = slice(b * LANES, (b + 1) * LANES)
         carried = gate_rows[...] * back_prop[:, col]
@@ -289,6 +289,8 @@
         up_v[:, col] = (carried * factor_b[:, col]).astype(BF16)
     for store in stores:
         store.start()
+    placed_out = pltpu.make_async_copy(place, place_out, store_sem.at[2])
+    placed_out.start()
     ring(dp - 2, False)
 
     whole(slot_in, slot_recv)
@@ -305,6 +307,7 @@
         ).start()
     pltpu.make_async_copy(pack_out.at[me_n], pack_in.at[me_n], pack_recv).start()
 
+    downs = []
     partial_of(dp - 1)
     for sub in range(SUBS):
         at = slice(sub * sub_rows, (sub + 1) * sub_rows)
@@ -312,27 +315,24 @@
             copy_of(dp - 2, half, sub, peer).wait_recv()
             value = part_sum[half, at, :] + part_in[dp - 2, half, at, :].astype(F32)
             down_v[at, half * LANES : (half + 1) * LANES] = value.astype(BF16)
-    last = pltpu.make_async_copy(down_v, down_out, store_sem.at[2])
-    last.start()
+        sends = pltpu.make_async_copy(
+            down_v.at[pl.ds(sub * sub_rows, sub_rows)],
+            down_out.at[pl.ds(sub * sub_rows, sub_rows)],
+            down_sem.at[sub],
+        )
+        sends.start()
+        downs.append(sends)
 
     whole(pack_in, pack_recv)
-    back_rows = jnp.sum(pack_in[...], axis=0)
-    for k in range(top):
-        named = routes_pad[k : k + 1, :]
-        lane = (named & (narrow - 1)) * wide + (named >> 3)
-        one = jnp.where(lane == expert_row, 1.0, 0.0)
-        got = jnp.dot(
-            back_rows, one, precision=lax.Precision.HIGHEST, preferred_element_type=F32
-        )
-        value = jnp.where(place[k : k + 1, :] == 0.0, got[0:1, :], got[1:2, :])
-        droute_v[k : k + 1, :] = value[:, 0:tok]
-    routed = pltpu.make_async_copy(droute_v, droute_out, store_sem.at[3])
-    routed.start()
+    packs = pltpu.make_async_copy(pack_in, pack_res, store_sem.at[3])
+    packs.start()
 
     for store in stores:
         store.wait()
-    last.wait()
-    routed.wait()
+    placed_out.wait()
+    packs.wait()
+    for send in downs:
+        send.wait()
     peers_n, peers_w = pl.ds(0, narrow - 1), pl.ds(0, wide - 1)
     for step in range(dp):
         whole(gathered.at[step, peers_n], token_send)
@@ -344,16 +344,28 @@
     whole(part_in, part_send)
 
 
-def hand_on(*refs):
-    sources, targets, held = refs[0:4], refs[4:8], refs[8:12]
-    taken, given = refs[12:]
-    reads = [pltpu.make_async_copy(a, b, taken.at[k]) for k, (a, b) in enumerate(zip(sources, held))]
-    writes = [pltpu.make_async_copy(a, b, given.at[k]) for k, (a, b) in enumerate(zip(held, targets))]
+def hand_on(wide, narrow, *refs):
+    sources, small, targets, route_out = refs[0:3], refs[3:6], refs[6:9], refs[9]
+    held, result, taken, given = refs[10:13], refs[13], refs[14], refs[15]
+    pack, place, routes = held
+    writes = [
+        pltpu.make_async_copy(a, b, given.at[k])
+        for k, (a, b) in enumerate([*zip(sources, targets), (result, route_out)])
+    ]
+    reads = [pltpu.make_async_copy(a, b, taken.at[k]) for k, (a, b) in enumerate(zip(small, held))]
+    for copy in reads + writes[:3]:
+        copy.start()
     for read in reads:
-        read.start()
-    for read, write in zip(reads, writes):
         read.wait()
-        write.start()
+    top, tok = result.shape
+    rows = jnp.sum(pack[...], axis=0)
+    for k in range(top):
+        named = routes[k : k + 1, :]
+        lane = (named & (narrow - 1)) * wide + (named >> 3)
+        one = jnp.where(lane == iota((LANES, tok), 0), 1.0, 0.0)
+        got = jnp.dot(rows, one, precision=lax.Precision.HIGHEST, preferred_element_type=F32)
+        result[k : k + 1, :] = jnp.where(place[k : k + 1, 0:tok] == 0.0, got[0:1, :], got[1:2, :])
+    writes[3].start()
     for write in writes:
         write.wait()
 
@@ -366,16 +378,18 @@
     dims = (dp, wide, narrow, tok, top, feat, hid, slots)
     vmem, dma = pltpu.VMEM, pltpu.SemaphoreType.DMA
     any_spec = pl.BlockSpec(memory_space=pl.ANY)
+    inputs = (out_grad, routes.T, gates.T, pre_gate[0, 0], pre_up[0, 0], down_weight[0])
     made = pl.pallas_call(
         functools.partial(kernel, dims),
         out_shape=(
-            jax.ShapeDtypeStruct((hid, feat // dp), BF16),
-            jax.ShapeDtypeStruct((slots, hid), BF16),
-            jax.ShapeDtypeStruct((slots, hid), BF16),
-            jax.ShapeDtypeStruct((top, tok), F32),
+            vmem((hid, feat // dp), BF16),
+            vmem((slots, hid), BF16),
+            vmem((slots, hid), BF16),
+            vmem((narrow, 2, LANES), F32),
+            vmem((top, LANES), F32),
         ),
         in_specs=[any_spec] * 6,
-        out_specs=(any_spec,) * 4,
+        out_specs=(any_spec,) * 5,
         scratch_shapes=[
             vmem((top, tok), jnp.int32),
             vmem((top, tok), BF16),
@@ -405,7 +419,6 @@
             vmem((dp - 1, 2, hid, LANES), BF16),
             vmem((2, hid, LANES), F32),
             vmem((hid, 2 * LANES), BF16),
-            vmem((top, tok), F32),
             vmem((wide, 1, LANES), F32),
             vmem((wide, 1, LANES), F32),
             vmem((narrow, 2, LANES), F32),
@@ -428,18 +441,29 @@
             dma,
             dma,
             dma((4,)),
+            dma((SUBS,)),
         ],
         compiler_params=pltpu.CompilerParams(collective_id=0, has_side_effects=True),
         name="routed_backward",
-    )(out_grad, routes.T, gates.T, pre_gate[0, 0], pre_up[0, 0], down_weight[0])
+    )(*inputs)
+    big = made[:3]
     down, dgate, dup, droute = pl.pallas_call(
-        hand_on,
-        out_shape=tuple(jax.ShapeDtypeStruct(a.shape, a.dtype) for a in made),
-        in_specs=[any_spec] * 4,
+        functools.partial(hand_on, wide, narrow),
+        out_shape=tuple(jax.ShapeDtypeStruct(a.shape, a.dtype) for a in big)
+        + (jax.ShapeDtypeStruct((top, tok), F32),),
+        in_specs=[any_spec] * 6,
         out_specs=(any_spec,) * 4,
-        scratch_shapes=[vmem(a.shape, a.dtype) for a in made] + [dma((4,)), dma((4,))],
+        scratch_shapes=[
+            vmem((narrow, 2, LANES), F32),
+            vmem((top, LANES), F32),
+            vmem((top, tok), jnp.int32),
+            vmem((top, tok), F32),
+            dma((3,)),
+            dma((4,)),
+        ],
+        compiler_params=pltpu.CompilerParams(vmem_limit_bytes=8 << 20),
         name="hand_on",
-    )(*made)
+    )(*made, routes.T)
     return down[None], dgate[None, None], dup[None, None], droute.T
 
 

time: 71.4 us -> 69.7 us (0.976)
  Pallas kernels: 69.8 us -> 68.2 us
    pallas_call x2, Pallas kernels: 69.8 us -> 68.2 us  [the longest x1 67 us: shards(): pl.pallas_call(functools.partial(kernel, dims), out_shape=(vmem((hid, fea...]
where the time goes in v3:
time: 69.7 us; the launch traced here: 68.8 us
  Pallas kernels  68.2 us (98%)
    pallas_call x1, Pallas kernels, shards(): pl.pallas_call(functools.partial(kernel, dims), out_shape=(vmem((hid, fea...  67 us

profile of v3, /device:TPU:1, one launch (start us, length us, event | category | flops | bytes accessed | tf_op | source)
XLA Modules:
  0.0 68.8 jit_solution(7814474230988635794)
XLA Ops:
  0.6 0.0 copy-start
  0.6 67.0 %routed_backward.1 = (bf16[768,256]{1,0:T(8,128)(2,1)S(1)}, bf16[256,768]{1,0:T(8,128)(2,1)S(1)}, bf16[256,768]{1,0:T(8,128)(2,1)S(1)}, f32[8,2,128]{2,1,0:T(2,128)S(1)}, f32[8,128]{1,0:T(8,128)S(1)}) custom-call(bf16[16,2048]{1,0:T(8,128)(2,1)} %grads_hbm.1, s32[8,16]{1,0:T(8,128)} %bitcast.9, bf16[8,16]{1,0:T(8,128)(2,1)} %bitcast.14, ...), custom_call_target="tpu_custom_call" | custom-call | tf_op jit(solution)/shard_map/routed_backward/pallas_call | solution.py:382
  67.6 0.0 copy-done
  67.6 1.2 %hand_on.1 = (bf16[768,256]{1,0:T(8,128)(2,1)}, bf16[256,768]{1,0:T(8,128)(2,1)}, bf16[256,768]{1,0:T(8,128)(2,1)}, f32[8,16]{1,0:T(8,128)}) custom-call(bf16[768,256]{1,0:T(8,128)(2,1)S(1)} %get-tuple-element.13.refs_0_, bf16[256,768]{1,0:T(8,128)(2,1)S(1)} %get-tuple-element.14.refs_1_, bf16[256,768]{1,0:T(8,128)(2,1)S(1)} %get-tuple-element.15.refs_2_, ...), custom_call_target="tpu_custom_call" | custom-call | tf_op jit(solution)/shard_map/hand_on/pallas_call | solution.py:450
Async XLA Ops:
  0.6 67.0 %copy-start = (s32[16,8]{0,1:T(8,128)S(1)}, s32[16,8]{0,1:T(8,128)}, u32[]{:S(2)}) copy-start(s32[16,8]{0,1:T(8,128)} %param.7) | copy-start | bytes 1540

commit v4 on v3

--- a/solution.py
+++ b/solution.py
@@ -244,9 +244,8 @@
         back_prop[...] = total
 
     arrive(0)
-    forward(2)
     ring(0, True)
-    pl.loop(3, 5)(forward)
+    pl.loop(2, 5)(forward)
     loads[2].wait()
     back(0)
 

time: 69.7 us -> 69.4 us (level)
  no operation moved by 1% of the time
where the time goes in v4:
time: 69.4 us; the launch traced here: 68.6 us
  Pallas kernels  67.9 us (98%)
    pallas_call x1, Pallas kernels, shards(): pl.pallas_call(functools.partial(kernel, dims), out_shape=(vmem((hid, fea...  66.7 us

profile of v4, /device:TPU:1, one launch (start us, length us, event | category | flops | bytes accessed | tf_op | source)
XLA Modules:
  0.0 68.6 jit_solution(16132356328769139436)
XLA Ops:
  0.6 0.0 copy-start
  0.6 66.7 %routed_backward.1 = (bf16[768,256]{1,0:T(8,128)(2,1)S(1)}, bf16[256,768]{1,0:T(8,128)(2,1)S(1)}, bf16[256,768]{1,0:T(8,128)(2,1)S(1)}, f32[8,2,128]{2,1,0:T(2,128)S(1)}, f32[8,128]{1,0:T(8,128)S(1)}) custom-call(bf16[16,2048]{1,0:T(8,128)(2,1)} %grads_hbm.1, s32[8,16]{1,0:T(8,128)} %bitcast.9, bf16[8,16]{1,0:T(8,128)(2,1)} %bitcast.14, ...), custom_call_target="tpu_custom_call" | custom-call | tf_op jit(solution)/shard_map/routed_backward/pallas_call | solution.py:381
  67.4 0.0 copy-done
  67.4 1.2 %hand_on.1 = (bf16[768,256]{1,0:T(8,128)(2,1)}, bf16[256,768]{1,0:T(8,128)(2,1)}, bf16[256,768]{1,0:T(8,128)(2,1)}, f32[8,16]{1,0:T(8,128)}) custom-call(bf16[768,256]{1,0:T(8,128)(2,1)S(1)} %get-tuple-element.13.refs_0_, bf16[256,768]{1,0:T(8,128)(2,1)S(1)} %get-tuple-element.14.refs_1_, bf16[256,768]{1,0:T(8,128)(2,1)S(1)} %get-tuple-element.15.refs_2_, ...), custom_call_target="tpu_custom_call" | custom-call | tf_op jit(solution)/shard_map/hand_on/pallas_call | solution.py:449
Async XLA Ops:
  0.6 66.7 %copy-start = (s32[16,8]{0,1:T(8,128)S(1)}, s32[16,8]{0,1:T(8,128)}, u32[]{:S(2)}) copy-start(s32[16,8]{0,1:T(8,128)} %param.7) | copy-start | bytes 1540
